TPU v7x, 512 devices: a whole 4x8x8 slice. The times are simulated.
512 devices in a mesh: aa: 8 (over x, core), ba: 8 (over y), col: 8 (over z).
Axes of the slice: x: 4, y: 8, z: 8, core: 2. Of those that a mesh axis runs over, the one named last changes fastest.
Arguments:
- field: float32 [192, 1024, 1024], P('col', 'aa', 'ba'), may hold values from -6 to 6
- factor: float32 [1024, 256], P('aa'), may hold values from -0.1875 to 0.1875
Outputs:
- gram: float32 [1024, 1024], P('ba', ('aa', 'col'))
All inputs are finite; a program needn't handle non-finite values.
Results may differ from a plain program's by a relative error of at most 0.000076.
Values sent between devices are 32-bit elements; how exact they have to be, the bound alone decides.
A program may use at most 64 MiB of HBM per device.

v0:
```python
import jax
import jax.numpy as jnp
from jax import lax
from jax.sharding import PartitionSpec as P


def shards(field, factor):
    ranks = factor.shape[1]
    depth = field.shape[0] * lax.axis_size("col")
    partial_core = jnp.einsum("kab,ar->krb", field, factor, precision=lax.Precision.HIGHEST)
    core = lax.psum_scatter(partial_core, "aa", scatter_dimension=1, tiled=True)
    block = jnp.einsum(
        "krb,krc->bc",
        core,
        lax.all_gather(core, "ba", axis=2, tiled=True),
        precision=lax.Precision.HIGHEST,
    )
    summed = lax.psum_scatter(block, ("aa", "col"), scatter_dimension=1, tiled=True)
    return summed / jnp.sqrt(jnp.float32(ranks * depth))


def solution(mesh):
    placed = (P("col", "aa", "ba"), P("aa", None))
    return jax.shard_map(
        shards, mesh=mesh, in_specs=placed, out_specs=P("ba", ("aa", "col")), check_vma=False
    )
```

profile of v0, /device:TPU:1, one launch (start us, length us, event | category | flops | bytes accessed | tf_op | source)
XLA Modules:
  0.0 326.9 jit_solution(14949219071277259198)
XLA Ops:
  6.5 0.0 copy-start
  6.5 0.0 reduce-scatter.2.cloned.1.call-start
  6.5 1.4 copy-done
  7.9 5.2 %convolution_bitcast_fusion = f32[24,256,128]{2,1,0:T(8,128)} fusion(f32[24,128,128]{2,1,0:T(8,128)S(1)} %copy-done, f32[128,256]{1,0:T(8,128)} %param.3), kind=kOutput, calls=%fused_computation | convolution fusion | flops 1207959552 | bytes 4849664 | tf_op jit(solution)/shard_map/kab,ar->krb/dot_general | solution.py:10
  13.2 0.0 reduce-scatter.2.cloned.1.call-update
  13.2 0.0 all-gather.2.cloned.1.call-start
  13.2 45.0 %reduce-scatter.2.cloned.1.call-done = f32[24,32,128]{2,1,0:T(8,128)} async-done(((f32[24,256,128]{2,1,0:T(8,128)}), f32[24,32,128]{2,1,0:T(8,128)}) %reduce-scatter.2.cloned.1.call-update) | async-done | bytes 393232 | tf_op jit(solution)/shard_map/reduce_scatter | solution.py:11
  58.2 0.0 all-gather.2.cloned.1.call-update
  58.2 0.0 all-reduce.3.cloned.1.call-start
  58.3 56.2 %all-gather.2.cloned.1.call-done = f32[24,32,1024]{2,1,0:T(8,128)} async-done(((f32[24,32,128]{2,1,0:T(8,128)}), f32[24,32,1024]{2,1,0:T(8,128)}) %all-gather.2.cloned.1.call-update) | async-done | bytes 3145744 | tf_op jit(solution)/shard_map/all_gather | solution.py:15
  114.5 7.9 %convolution_bitcast_fusion.1 = f32[128,1024]{0,1:T(8,128)} fusion(f32[24,32,128]{2,1,0:T(8,128)} %reduce-scatter.2.cloned.1.call-done, f32[24,32,1024]{2,1,0:T(8,128)} %all-gather.2.cloned.1.call-done), kind=kOutput, calls=%fused_computation.1 | convolution fusion | flops 1207959552 | bytes 4063232 | tf_op jit(solution)/shard_map/krb,krc->bc/dot_general | solution.py:12
  122.4 0.0 all-reduce.3.cloned.1.call-update
  122.4 1.3 dynamic-slice
  124.3 194.7 %all-reduce.3.cloned.1.call-done = f32[128,1024]{0,1:T(8,128)} async-done(((f32[128,1024]{0,1:T(8,128)}), f32[128,1024]{0,1:T(8,128)}) %all-reduce.3.cloned.1.call-update) | async-done | bytes 524304
  319.0 1.3 dynamic-slice_multiply_fusion
Async XLA Ops:
  6.5 1.4 copy-start
  6.5 51.7 %reduce-scatter.2.cloned.1.call-start = ((), (), s32[]{:S(2)}) async-start(), calls=%async_computation.1 | async-start | bytes 3538944 | tf_op jit(solution)/shard_map/reduce_scatter | solution.py:11
  13.2 101.3 %all-gather.2.cloned.1.call-start = ((), (), s32[]{:S(2)}) async-start(), calls=%async_computation.2 | async-start | bytes 3538944 | tf_op jit(solution)/shard_map/all_gather | solution.py:15
  58.2 260.8 %all-reduce.3.cloned.1.call-start = ((), (), s32[]{:S(2)}) async-start(), calls=%async_computation.3 | async-start | bytes 1048576
Sparse Core Ops, SparseCore 0:
  13.3 44.8 reduce-scatter.1
  60.2 54.2 all-gather.1
  122.5 196.4 all-reduce.2
where the time goes:
time: 328 us; the launch traced here: 327 us
  waiting for transfers between devices  296 us (90%)
  between operations  13.8 us (4%)
  matrix products  13.1 us (4%)
    unnamed x4, waiting for transfers between devices  195 us
    all_gather x1, waiting for transfers between devices, shards(): lax.all_gather(core, 'ba', axis=2, tiled=True)  56.2 us
    reduce_scatter x1, waiting for transfers between devices, shards(): core = lax.psum_scatter(partial_core, 'aa', scatter_dimension=1, tiled=True)  45 us
    dot_general x1, matrix products, shards(): jnp.einsum('krb,krc->bc', core, lax.all_gather(core, 'ba', axis=2, tiled=...  7.85 us
  transfers between devices with their start and end apart: 3, of which 3 were waited for; matrix products, arithmetic and copies ran while one was open for 0% of the time, Pallas kernels for 0%

commit v1 on v0

v1 whole, which is shorter than its diff:
```python
import jax
import jax.numpy as jnp
from jax import lax
from jax.experimental import pallas as pl
from jax.experimental.pallas import tpu as pltpu
from jax.sharding import PartitionSpec as P

MESH = pl.DeviceIdType.MESH
F32 = jnp.float32
BF16 = jnp.bfloat16
T = 128
RELS = (2, 1, 3, 0)
J = 3
HOPS = 4


def split(v):
    high = v.astype(BF16)
    return high, (v - high.astype(F32)).astype(BF16)


def lhs_of(v):
    high, low = split(v)
    return jnp.concatenate([high, low, high], axis=1)


def rhs_of(v):
    high, low = split(v)
    return jnp.concatenate([high, high, low], axis=0)


def kernel(scale, field, factor, out, f2, u2, w, xs, xr_, own, yr_, ol, g, g3, tx, gx, d_, dt, gz, gm,
           lsem, fs, fr, xss, xrs, yss, yrs, s3, r3, sx, rx, sz, rz, sm, rm, zsem):
    aa, y, z = lax.axis_index("aa"), lax.axis_index("ba"), lax.axis_index("col")
    core, x = aa % 2, aa // 2
    partner = aa + 1 - 2 * core
    right = ((x + 1) % 4) * 2 + core
    left = ((x + 3) % 4) * 2 + core
    up, down = (y + 1) % 8, (y + 7) % 8
    zup, zdown = (z + 1) % 8, (z + 7) % 8
    order = [(j, rel) for j in range(J) for rel in RELS]
    sent = []

    def slot(j, rel):
        return j * 4 + rel

    def remote(src, dst, send, recv, **where):
        return pltpu.make_async_remote_copy(
            src_ref=src, dst_ref=dst, send_sem=send, recv_sem=recv, device_id=where, device_id_type=MESH)

    def go(copy):
        copy.start()
        sent.append(copy)

    loads = {}
    fl = pltpu.make_async_copy(factor, u2.at[pl.ds(0, T)], lsem.at[12])
    fl.start()
    for j, rel in order:
        k = 12 * core + 3 * ((x + rel) % 4) + j
        loads[j, rel] = pltpu.make_async_copy(field.at[k], f2.at[slot(j, rel), pl.ds(0, T)], lsem.at[slot(j, rel)])
        loads[j, rel].start()

    barrier = pltpu.get_barrier_semaphore()
    for where in ({"aa": partner}, {"aa": right}, {"aa": left}, {"ba": up}, {"ba": down}, {"col": zup}, {"col": zdown}):
        pl.semaphore_signal(barrier, inc=1, device_id=where, device_id_type=MESH)
    pl.semaphore_wait(barrier, 7)

    def z_signal(i):
        for where in ({"col": zup}, {"col": zdown}):
            pl.semaphore_signal(zsem.at[i], inc=1, device_id=where, device_id_type=MESH)

    fx = remote(factor, u2.at[pl.ds(T, T)], fs.at[12], fr.at[12], aa=partner)
    go(fx)
    fields = {}
    for j, rel in order:
        k = 12 * (1 - core) + 3 * ((x + rel) % 4) + j
        fields[j, rel] = remote(field.at[k], f2.at[slot(j, rel), pl.ds(T, T)],
                                fs.at[slot(j, rel)], fr.at[slot(j, rel)], aa=partner)
        go(fields[j, rel])
    z_signal(0)

    fl.wait()
    fx.wait_recv()
    w[...] = lhs_of(u2[...].T)

    def product(j, rel):
        loads[j, rel].wait()
        fields[j, rel].wait_recv()
        return jnp.dot(w[...], rhs_of(f2[slot(j, rel)]), preferred_element_type=F32)

    xcopies = {}

    def xsend(kind, way, j):
        i = (kind * 2 + way) * J + j
        c = remote(xs.at[i], xr_.at[i], xss.at[i], xrs.at[i], aa=right if way == 0 else left)
        xcopies[kind, way, j] = c
        go(c)

    def xref(ref, kind, way, j):
        return ref.at[(kind * 2 + way) * J + j]

    def stage_ab(j):
        p = product(j, 2)
        xref(xs, 0, 0, j)[...] = p[:T]
        xref(xs, 0, 1, j)[...] = p[T:]
        xsend(0, 0, j)
        xsend(0, 1, j)
        p = product(j, 1)
        xref(xs, 1, 0, j)[...] = p[T:]
        xsend(1, 0, j)
        xref(xs, 2, 0, j)[...] = p[:T]
        p = product(j, 3)
        xref(xs, 1, 1, j)[...] = p[:T]
        xsend(1, 1, j)
        xref(xs, 2, 1, j)[...] = p[T:]

    def stage_c(j):
        for way in (0, 1):
            xcopies[0, way, j].wait_recv()
            xref(xs, 2, way, j)[...] += xref(xr_, 0, way, j)[...]
            xsend(2, way, j)
        p = product(j, 0)
        own[2 * j] = p[:T]
        own[2 * j + 1] = p[T:]

    ycopies = {}

    def ysend(d, h, j):
        i = (h * J + j) * HOPS + d - 1
        target = up if h == 0 else down
        src = own.at[2 * j + h] if d == 1 else yr_.at[i - 1]
        dst = yr_.at[i]
        if d == HOPS:
            part = target // 4
            src, dst = src.at[pl.ds(part * 64, 64)], dst.at[pl.ds(0, 64)]
        c = remote(src, dst, yss.at[i], yrs.at[i], ba=target)
        ycopies[d, h, j] = c
        go(c)

    def add_gram(e, v, first):
        if first:
            g[e] = v
        else:
            g[e] += v

    def stage_total(j):
        xcopies[1, 0, j].wait_recv()
        xcopies[1, 1, j].wait_recv()
        for h in (0, 1):
            xcopies[2, h, j].wait_recv()
            own[2 * j + h] = own[2 * j + h] + (xref(xr_, 2, h, j)[...] + xref(xr_, 1, 1 - h, j)[...])
            ysend(1, h, j)

    def gram0(j):
        for h in (0, 1):
            v = own[2 * j + h]
            ol[2 * j + h] = lhs_of(v.T)
            add_gram(0, jnp.dot(ol[2 * j + h], rhs_of(v), preferred_element_type=F32), j == 0 and h == 0)

    def stage_hop(j, d):
        for h in (0, 1):
            ycopies[d, h, j].wait_recv()
            if d < HOPS:
                ysend(d + 1, h, j)
        for h in (0, 1):
            i = (h * J + j) * HOPS + d - 1
            e = (8 - d) % 8 if h == 0 else d
            if d < HOPS:
                v = jnp.dot(ol[2 * j + h], rhs_of(yr_[i]), preferred_element_type=F32)
            else:
                mine = own[2 * j + h, pl.ds((y // 4) * 64, 64), :]
                v = jnp.dot(lhs_of(mine.T), rhs_of(yr_[i, pl.ds(0, 64), :]), preferred_element_type=F32)
            add_gram(e, v, j == 0 and (d < HOPS or h == 0))

    def z_round(i):
        pl.semaphore_wait(zsem.at[i], 2)
        if i < 2:
            z_signal(i + 1)

    stage_ab(0)
    stage_c(0)
    z_round(0)
    stage_ab(1)
    stage_total(0)
    stage_c(1)
    z_round(1)
    stage_ab(2)
    gram0(0)
    stage_hop(0, 1)
    stage_total(1)
    stage_c(2)
    z_round(2)
    gram0(1)
    stage_hop(0, 2)
    stage_hop(1, 1)
    stage_total(2)
    stage_hop(0, 3)
    stage_hop(1, 2)
    gram0(2)
    stage_hop(2, 1)
    stage_hop(0, 4)
    stage_hop(1, 3)
    stage_hop(2, 2)
    stage_hop(1, 4)
    stage_hop(2, 3)
    stage_hop(2, 4)

    pair = {}
    for rel in RELS:
        o = (x + rel) % 4
        theirs = 2 * o + 1 - core
        pair[rel] = remote(g.at[(theirs - y + 8) % 8], g3.at[rel], s3.at[rel], r3.at[rel], aa=partner)
        go(pair[rel])
    across = {}
    for rel in RELS:
        o = (x + rel) % 4
        pair[rel].wait_recv()
        tx[rel] = g[(2 * o + core - y + 8) % 8] + g3[rel]
        if rel:
            across[rel] = remote(tx.at[rel], gx.at[rel], sx.at[rel], rx.at[rel], aa=2 * o + core)
            go(across[rel])
    total = tx[0]
    for rel in (1, 3, 2):
        across[rel].wait_recv()
        total = total + gx[rel]
    d_[...] = total
    dt[...] = total.T

    def mirror(dz):
        zt = (z + dz) % 8
        return remote(d_.at[pl.ds(zt * 16, 16)], gm.at[dz], sm.at[dz], rm.at[dz], aa=y, ba=aa, col=zt)

    @pl.when(aa != y)
    def _():
        for dz in (4, 3, 5, 2, 6, 1, 7, 0):
            mirror(dz).start()

    line = {}
    for dz in (4, 3, 5, 2, 6, 1, 7):
        zt = (z + dz) % 8
        line[dz] = remote(dt.at[pl.ds(zt * 16, 16)], gz.at[dz], sz.at[dz], rz.at[dz], col=zt)
        go(line[dz])
    result = dt[pl.ds(z * 16, 16), :]
    for dz in (1, 7, 2, 6, 3, 5, 4):
        line[dz].wait_recv()
        result = result + gz[dz]
    out[...] = result * scale

    @pl.when(aa != y)
    def _():
        other = None
        for dz in (0, 1, 7, 2, 6, 3, 5, 4):
            mirror(dz).wait_recv()
            other = gm[dz] if other is None else other + gm[dz]
        out[...] += other * scale
        for dz in range(8):
            mirror(dz).wait_send()

    for c in sent:
        c.wait_send()


def shards(field, factor):
    ranks = factor.shape[1]
    depth = field.shape[0] * lax.axis_size("col")
    scale = float((ranks * depth) ** -0.5)
    tile = (T, T)
    dma = pltpu.SemaphoreType.DMA
    vmem = pltpu.VMEM

    def body(*refs):
        kernel(scale, *refs)

    ny = 2 * J * HOPS
    result = pl.pallas_call(
        body,
        out_shape=jax.ShapeDtypeStruct((16, T), F32),
        in_specs=[pl.BlockSpec(memory_space=pl.ANY)] * 2,
        out_specs=pl.BlockSpec(memory_space=pltpu.VMEM),
        scratch_shapes=[
            vmem((12, 2 * T, T), F32), vmem((2 * T, 2 * T), F32), vmem((2 * T, 6 * T), BF16),
            vmem((18,) + tile, F32), vmem((18,) + tile, F32),
            vmem((2 * J,) + tile, F32), vmem((ny,) + tile, F32), vmem((2 * J, T, 3 * T), BF16),
            vmem((8,) + tile, F32), vmem((4,) + tile, F32), vmem((4,) + tile, F32), vmem((4,) + tile, F32),
            vmem(tile, F32), vmem(tile, F32), vmem((8, 16, T), F32), vmem((8, 16, T), F32),
            dma((13,)), dma((13,)), dma((13,)), dma((18,)), dma((18,)), dma((ny,)), dma((ny,)),
            dma((4,)), dma((4,)), dma((4,)), dma((4,)), dma((8,)), dma((8,)), dma((8,)), dma((8,)),
            pltpu.SemaphoreType.REGULAR((3,)),
        ],
        compiler_params=pltpu.CompilerParams(collective_id=0, has_side_effects=True),
    )(field, factor)
    return result.T


def solution(mesh):
    placed = (P("col", "aa", "ba"), P("aa", None))
    return jax.shard_map(
        shards, mesh=mesh, in_specs=placed, out_specs=P("ba", ("aa", "col")), check_vma=False
    )
```

time: 328 us -> 68.7 us (0.21)
  waiting for transfers between devices: 296 us -> 0 us
  Pallas kernels: 0 us -> 67.3 us
  between operations: 13.8 us -> 0.01 us
  matrix products: 13.1 us -> 0 us
    unnamed x4 -> x0, waiting for transfers between devices: 195 us -> none
    pallas_call x0 -> x1, Pallas kernels: none -> 67.3 us  [shards(): pl.pallas_call(body, out_shape=jax.ShapeDtypeStruct((16, T), F32), in_spe...]
    all_gather x1 -> x0, waiting for transfers between devices: 56.2 us -> none  [shards(): lax.all_gather(core, 'ba', axis=2, tiled=True)]
    reduce_scatter x1 -> x0, waiting for transfers between devices: 45 us -> none  [shards(): core = lax.psum_scatter(partial_core, 'aa', scatter_dimension=1, tiled=True)]
    dot_general x2 -> x0, matrix products: 13.1 us -> none  [the longest x1 7.85 us: shards(): jnp.einsum('krb,krc->bc', core, lax.all_gather(core, 'ba', axis=2, tiled=...]
  transfers between devices with their start and end apart: 3 -> 0, of which waited for: 3 -> 0; matrix products, arithmetic and copies ran while one was open for 0% -> 0% of each run, Pallas kernels for 0% -> 0%
where the time goes in v1:
time: 68.7 us; the launch traced here: 68.6 us
  Pallas kernels  67.3 us (98%)
  local copies, waits for them, and re-layouts  1.3 us (2%)
    pallas_call x1, Pallas kernels, shards(): pl.pallas_call(body, out_shape=jax.ShapeDtypeStruct((16, T), F32), in_spe...  67.3 us

profile of v1, /device:TPU:1, one launch (start us, length us, event | category | flops | bytes accessed | tf_op | source)
XLA Modules:
  0.0 68.6 jit_solution(593748405036352081)
XLA Ops:
  0.0 67.3 %shard_map.28 = f32[16,128]{1,0:T(8,128)} custom-call(f32[24,128,128]{2,1,0:T(8,128)} %refs_0_.1, f32[128,256]{1,0:T(8,128)} %refs_1_.1), custom_call_target="tpu_custom_call" | custom-call | tf_op jit(solution)/shard_map/pallas_call | solution.py:275
  67.3 1.3 %copy.4 = f32[128,16]{0,1:T(8,128)} copy(f32[128,16]{0,1:T(8,128)} %bitcast.1) | data formatting | bytes 16384

commit v2 on v0

v2 whole, which is shorter than its diff:
```python
import jax
import jax.numpy as jnp
from jax import lax
from jax.experimental import pallas as pl
from jax.experimental.pallas import tpu as pltpu
from jax.sharding import PartitionSpec as P

MESH = pl.DeviceIdType.MESH
F32 = jnp.float32
BF16 = jnp.bfloat16
T = 128
K = 3
S = 2
R = T // S
Q = R // 2
HOPS = 4
RELS = (2, 1, 3, 0)
PAIRS = ((2, 7), (6, 1), (0, 3), (4, 5))
TREE = {(0, 0): 4, (0, 1): 4, (1, 0): 4, (1, 1): 3, (2, 0): 3, (2, 1): 3}
FORWARD = {
    4: {0: (1,), 1: (2,), 2: (3,), 3: (4,)},
    3: {0: (1,), 1: (2,), 2: (4, 3)},
    2: {0: (1, 2), 2: (4, 3)},
}
ORDER = (
    ("W",), ("PA", 0), ("SA", 0, 0), ("SA", 0, 1), ("PB", 0), ("SB", 0, 0),
    ("SB", 0, 1), ("PS", 0), ("Z", 0), ("PA", 1), ("PB", 1), ("PS", 1),
    ("PA", 2), ("SA", 1, 0), ("PB", 2), ("Z", 1), ("SB", 1, 0), ("PS", 2),
    ("C", 0, 0), ("C", 0, 1), ("Z", 2), ("SA", 1, 1), ("SB", 1, 1), ("C", 1, 0),
    ("SA", 2, 0), ("T", 0, 0), ("SB", 2, 0), ("T", 0, 1), ("N", 0), ("SA", 2, 1),
    ("C", 1, 1), ("SB", 2, 1), ("T", 1, 0), ("C", 2, 0), ("H", 0, 0, 1), ("H", 0, 1, 1),
    ("G", 0, 1), ("C", 2, 1), ("T", 1, 1), ("N", 1), ("H", 1, 0, 1), ("T", 2, 0),
    ("H", 0, 0, 2), ("H", 0, 1, 2), ("G", 0, 2), ("T", 2, 1), ("N", 2), ("H", 1, 1, 1),
    ("G", 1, 1), ("H", 1, 0, 2), ("H", 2, 0, 1), ("H", 0, 0, 3), ("H", 0, 1, 3), ("G", 0, 3),
    ("H", 2, 1, 1), ("G", 2, 1), ("H", 1, 1, 2), ("G", 1, 2), ("H", 1, 0, 3), ("H", 2, 0, 2),
    ("G", 0, 4), ("H", 2, 1, 2), ("G", 2, 2), ("P1", 0), ("P1", 1), ("P2", 0),
    ("P2", 1), ("G", 1, 3), ("G", 1, 4), ("G", 2, 3), ("P1", 2), ("G", 2, 4),
    ("P1", 3), ("P2", 2), ("P2", 3),
)


def split(v):
    high = v.astype(BF16)
    return high, (v - high.astype(F32)).astype(BF16)


def lhs_of(v):
    high, low = split(v)
    return jnp.concatenate([high, low, high], axis=1)


def rhs_of(v):
    high, low = split(v)
    return jnp.concatenate([high, high, low], axis=0)


def dot(a, b):
    return jnp.dot(a, b, preferred_element_type=F32)


def kernel(scale, field, factor, out, f2, u2, w, xs, xr, own, yr, ol, g, g3, tx, tt, mine, gz, gm,
           lsem, fs, fr, xss, xrs, yss, yrs, s3, r3, sz, rz, sm, rm, zsem):
    aa, y, z = lax.axis_index("aa"), lax.axis_index("ba"), lax.axis_index("col")
    core, x = aa % 2, aa // 2
    partner = aa + 1 - 2 * core
    right = ((x + 1) % 4) * 2 + core
    left = ((x + 3) % 4) * 2 + core
    up, down = (y + 1) % 8, (y + 7) % 8
    zup, zdown = (z + 1) % 8, (z + 7) % 8
    slots = [(k, rel) for k in range(K) for rel in RELS]
    sent = []

    def remote(src, dst, send, recv, **where):
        return pltpu.make_async_remote_copy(
            src_ref=src, dst_ref=dst, send_sem=send, recv_sem=recv, device_id=where, device_id_type=MESH)

    def go(copy):
        copy.start()
        sent.append(copy)
        return copy

    loads = {}
    load_factor = pltpu.make_async_copy(factor, u2.at[pl.ds(0, T)], lsem.at[12])
    load_factor.start()
    for i, (k, rel) in enumerate(slots):
        kk = 12 * core + 3 * ((x + rel) % 4) + k
        loads[k, rel] = pltpu.make_async_copy(field.at[kk], f2.at[i, pl.ds(0, T)], lsem.at[i])
        loads[k, rel].start()

    barrier = pltpu.get_barrier_semaphore()
    for where in ({"aa": partner}, {"aa": right}, {"aa": left}, {"ba": up}, {"ba": down}, {"col": zup}, {"col": zdown}):
        pl.semaphore_signal(barrier, inc=1, device_id=where, device_id_type=MESH)
    pl.semaphore_wait(barrier, 7)

    def z_signal(i):
        for where in ({"col": zup}, {"col": zdown}):
            pl.semaphore_signal(zsem.at[i], inc=1, device_id=where, device_id_type=MESH)

    swap_factor = go(remote(factor, u2.at[pl.ds(T, T)], fs.at[12], fr.at[12], aa=partner))
    fields = {}
    for i, (k, rel) in enumerate(slots):
        kk = 12 * (1 - core) + 3 * ((x + rel) % 4) + k
        fields[k, rel] = go(remote(field.at[kk], f2.at[i, pl.ds(T, T)], fs.at[i], fr.at[i], aa=partner))
    z_signal(0)

    xcopies, ycopies, pairs, waited = {}, {}, {}, set()

    def xat(kind, way, k):
        return (kind * 2 + way) * K + k

    def yat(h, k, d):
        return (h * K + k) * HOPS + d - 1

    def xsend(kind, way, k, s):
        i = xat(kind, way, k)
        rows = pl.ds(s * R, R)
        xcopies[kind, way, k, s] = go(remote(xs.at[i, rows], xr.at[i, rows], xss.at[i * S + s], xrs.at[i * S + s],
                                             aa=right if way == 0 else left))

    def ysend(h, k, s, base):
        for d in FORWARD[TREE[k, s]].get(base, ()):
            i = yat(h, k, d)
            target = (y + (d - base if h == 0 else 8 - d + base)) % 8
            src = own.at[2 * k + h] if base == 0 else yr.at[yat(h, k, base)]
            if d < HOPS:
                src, dst = src.at[pl.ds(s * R, R)], yr.at[i, pl.ds(s * R, R)]
            else:
                src, dst = src.at[pl.ds(s * R + (target // 4) * Q, Q)], yr.at[i, pl.ds(s * Q, Q)]
            ycopies[h, k, s, d] = go(remote(src, dst, yss.at[i * S + s], yrs.at[i * S + s], ba=target))

    def arrived(h, k, s, d):
        if (h, k, s, d) not in waited:
            waited.add((h, k, s, d))
            ycopies[h, k, s, d].wait_recv()

    def product(k, rel):
        loads[k, rel].wait()
        fields[k, rel].wait_recv()
        return dot(w[...], rhs_of(f2[slots.index((k, rel))]))

    def add_gram(e, v, first):
        if first:
            g[e] = v
        else:
            g[e] += v

    def step_w():
        load_factor.wait()
        swap_factor.wait_recv()
        w[...] = lhs_of(u2[...].T)

    def step_pa(k):
        p = product(k, 2)
        xs[xat(0, 0, k)] = p[:T]
        xs[xat(0, 1, k)] = p[T:]

    def step_pb(k):
        p = product(k, 1)
        xs[xat(1, 0, k)] = p[T:]
        xs[xat(2, 0, k)] = p[:T]
        p = product(k, 3)
        xs[xat(1, 1, k)] = p[:T]
        xs[xat(2, 1, k)] = p[T:]

    def step_ps(k):
        p = product(k, 0)
        own[2 * k] = p[:T]
        own[2 * k + 1] = p[T:]

    def step_sa(k, s):
        xsend(0, 0, k, s)
        xsend(0, 1, k, s)

    def step_sb(k, s):
        xsend(1, 0, k, s)
        xsend(1, 1, k, s)

    def step_c(k, s):
        rows = pl.ds(s * R, R)
        for way in (0, 1):
            xcopies[0, way, k, s].wait_recv()
            xs[xat(2, way, k), rows, :] += xr[xat(0, way, k), rows, :]
            xsend(2, way, k, s)

    def step_t(k, s):
        rows = pl.ds(s * R, R)
        for h in (0, 1):
            xcopies[1, 1 - h, k, s].wait_recv()
            xcopies[2, h, k, s].wait_recv()
            own[2 * k + h, rows, :] += xr[xat(2, h, k), rows, :] + xr[xat(1, 1 - h, k), rows, :]
            ysend(h, k, s, 0)

    def step_h(k, s, d):
        for h in (0, 1):
            arrived(h, k, s, d)
        for h in (0, 1):
            ysend(h, k, s, d)

    def step_n(k):
        for h in (0, 1):
            v = own[2 * k + h]
            ol[2 * k + h] = lhs_of(v.T)
            add_gram(0, dot(ol[2 * k + h], rhs_of(v)), k == 0 and h == 0)

    def step_g(k, d):
        for h in (0, 1):
            i = yat(h, k, d)
            for s in range(S):
                arrived(h, k, s, d)
            if d < HOPS:
                v = dot(ol[2 * k + h], rhs_of(yr[i]))
            else:
                local = jnp.concatenate([own[2 * k + h, pl.ds(s * R + (y // 4) * Q, Q), :] for s in range(S)], axis=0)
                v = dot(lhs_of(local.T), rhs_of(yr[i, pl.ds(0, S * Q), :]))
            add_gram((8 - d) % 8 if h == 0 else d, v, k == 0 and (d < HOPS or h == 0))

    def step_z(i):
        pl.semaphore_wait(zsem.at[i], 2)
        if i < 2:
            z_signal(i + 1)

    def choose(p):
        a, b = PAIRS[p]
        t = (y + a + core) % 2
        return a * (1 - t) + b * t, a * t + b * (1 - t)

    def step_p1(p):
        pairs[p] = go(remote(g.at[choose(p)[1]], g3.at[p], s3.at[p], r3.at[p], aa=partner))

    def line(p, o, dz):
        zt, i = (z + 8 - dz) % 8, ((x - o + 4) % 4) * 8 + dz
        return remote(tt.at[p, pl.ds(zt * 16, 16)], gz.at[i], sz.at[p * 8 + dz], rz.at[i], aa=2 * o + core, col=zt)

    def mirror(p, c, dz):
        zt, i = (z + 8 - dz) % 8, ((x - y // 2 + 4) % 4) * 8 + dz
        return remote(tx.at[p, pl.ds(zt * 16, 16)], gm.at[i], sm.at[p * 8 + dz], rm.at[i], aa=y, ba=c, col=zt)

    def spread(p, act):
        kept = choose(p)[0]
        c = (y + kept) % 8
        far = (4, 3, 5, 2, 6, 1, 7)

        def mirrors():
            for dz in far + (0,):
                act(mirror(p, c, dz))

        if 0 in PAIRS[p]:
            pl.when(kept != 0)(mirrors)
        else:
            mirrors()
        for dz in far:
            act(line(p, c // 2, dz))

        @pl.when(c // 2 != x)
        def _():
            act(line(p, c // 2, 0))

    def step_p2(p):
        kept = choose(p)[0]
        pairs[p].wait_recv()
        total = g[kept] + g3[p]
        tx[p] = total
        tt[p] = total.T
        spread(p, lambda copy: copy.start())

        @pl.when((y + kept) % 8 == aa)
        def _():
            mine[...] = tt[p, pl.ds(z * 16, 16), :]

    steps = {"W": step_w, "PA": step_pa, "PB": step_pb, "PS": step_ps, "SA": step_sa, "SB": step_sb, "C": step_c,
             "T": step_t, "H": step_h, "N": step_n, "G": step_g, "Z": step_z, "P1": step_p1, "P2": step_p2}
    for name, *where in ORDER:
        steps[name](*where)

    result = mine[...]
    for i in range(1, 32):
        remote(tt.at[0, pl.ds(0, 16)], gz.at[i], sz.at[0], rz.at[i], aa=right).wait_recv()
        result = result + gz[i]
    out[...] = result * scale

    @pl.when(aa != y)
    def _():
        other = None
        for i in range(32):
            remote(tx.at[0, pl.ds(0, 16)], gm.at[i], sm.at[0], rm.at[i], aa=right).wait_recv()
            other = gm[i] if other is None else other + gm[i]
        out[...] += other * scale

    for p in range(4):
        spread(p, lambda copy: copy.wait_send())
    for c in sent:
        c.wait_send()


def shards(field, factor):
    ranks = factor.shape[1]
    depth = field.shape[0] * lax.axis_size("col")
    scale = float((ranks * depth) ** -0.5)
    tile = (T, T)
    dma = pltpu.SemaphoreType.DMA
    vmem = pltpu.VMEM

    def body(*refs):
        kernel(scale, *refs)

    nx, ny = 6 * K, 2 * K * HOPS
    result = pl.pallas_call(
        body,
        out_shape=jax.ShapeDtypeStruct((16, T), F32),
        in_specs=[pl.BlockSpec(memory_space=pl.ANY)] * 2,
        out_specs=pl.BlockSpec(memory_space=pltpu.VMEM),
        scratch_shapes=[
            vmem((12, 2 * T, T), F32), vmem((2 * T, 2 * T), F32), vmem((2 * T, 6 * T), BF16),
            vmem((nx,) + tile, F32), vmem((nx,) + tile, F32),
            vmem((2 * K,) + tile, F32), vmem((ny,) + tile, F32), vmem((2 * K, T, 3 * T), BF16),
            vmem((8,) + tile, F32), vmem((4,) + tile, F32), vmem((4,) + tile, F32), vmem((4,) + tile, F32),
            vmem((16, T), F32), vmem((32, 16, T), F32), vmem((32, 16, T), F32),
            dma((13,)), dma((13,)), dma((13,)), dma((nx * S,)), dma((nx * S,)), dma((ny * S,)), dma((ny * S,)),
            dma((4,)), dma((4,)), dma((32,)), dma((32,)), dma((32,)), dma((32,)),
            pltpu.SemaphoreType.REGULAR((3,)),
        ],
        compiler_params=pltpu.CompilerParams(collective_id=0, has_side_effects=True),
    )(field, factor)
    return result.T


def solution(mesh):
    placed = (P("col", "aa", "ba"), P("aa", None))
    return jax.shard_map(
        shards, mesh=mesh, in_specs=placed, out_specs=P("ba", ("aa", "col")), check_vma=False
    )
```

time: 328 us -> 59.6 us (0.18)
  the two profiles are of different devices: /device:TPU:1 before, /device:TPU:4 now
where the time goes in v2:
time: 59.6 us; the launch traced here: 59.5 us
  Pallas kernels  58.2 us (98%)
  local copies, waits for them, and re-layouts  1.3 us (2%)
    pallas_call x1, Pallas kernels, shards(): pl.pallas_call(body, out_shape=jax.ShapeDtypeStruct((16, T), F32), in_spe...  58.2 us
    unnamed x1, local copies, waits for them, and re-layouts  1.3 us

profile of v2, /device:TPU:4, one launch (start us, length us, event | category | flops | bytes accessed | tf_op | source)
XLA Modules:
  0.0 59.5 jit_solution(1388281170612643267)
XLA Ops:
  0.0 58.2 %shard_map.28 = f32[16,128]{1,0:T(8,128)} custom-call(f32[24,128,128]{2,1,0:T(8,128)} %refs_0_.1, f32[128,256]{1,0:T(8,128)} %refs_1_.1), custom_call_target="tpu_custom_call" | custom-call | tf_op jit(solution)/shard_map/pallas_call | solution.py:307
  58.2 1.3 %copy.4 = f32[128,16]{0,1:T(8,128)} copy(f32[128,16]{0,1:T(8,128)} %bitcast.1) | data formatting | bytes 16384

commit v3 on v2

--- a/solution.py
+++ b/solution.py
@@ -34,8 +34,8 @@
     ("G", 1, 1), ("H", 1, 0, 2), ("H", 2, 0, 1), ("H", 0, 0, 3), ("H", 0, 1, 3), ("G", 0, 3),
     ("H", 2, 1, 1), ("G", 2, 1), ("H", 1, 1, 2), ("G", 1, 2), ("H", 1, 0, 3), ("H", 2, 0, 2),
     ("G", 0, 4), ("H", 2, 1, 2), ("G", 2, 2), ("P1", 0), ("P1", 1), ("P2", 0),
-    ("P2", 1), ("G", 1, 3), ("G", 1, 4), ("G", 2, 3), ("P1", 2), ("G", 2, 4),
-    ("P1", 3), ("P2", 2), ("P2", 3),
+    ("P2", 1), ("G", 1, 3), ("G", 1, 4), ("G", 2, 3), ("G", 2, 4), ("P1", 3),
+    ("P1", 2), ("P2", 3), ("P2", 2),
 )
 
 
@@ -235,33 +235,37 @@
         zt, i = (z + 8 - dz) % 8, ((x - y // 2 + 4) % 4) * 8 + dz
         return remote(tx.at[p, pl.ds(zt * 16, 16)], gm.at[i], sm.at[p * 8 + dz], rm.at[i], aa=y, ba=c, col=zt)
 
-    def spread(p, act):
+    far = (4, 3, 5, 2, 6, 1, 7)
+
+    def mirrors(p, act):
         kept = choose(p)[0]
-        c = (y + kept) % 8
-        far = (4, 3, 5, 2, 6, 1, 7)
-
-        def mirrors():
+
+        def each():
             for dz in far + (0,):
-                act(mirror(p, c, dz))
+                act(mirror(p, (y + kept) % 8, dz))
 
         if 0 in PAIRS[p]:
-            pl.when(kept != 0)(mirrors)
+            pl.when(kept != 0)(each)
         else:
-            mirrors()
+            each()
+
+    def lines(p, act):
+        o = ((y + choose(p)[0]) % 8) // 2
         for dz in far:
-            act(line(p, c // 2, dz))
-
-        @pl.when(c // 2 != x)
+            act(line(p, o, dz))
+
+        @pl.when(o != x)
         def _():
-            act(line(p, c // 2, 0))
+            act(line(p, o, 0))
 
     def step_p2(p):
         kept = choose(p)[0]
         pairs[p].wait_recv()
         total = g[kept] + g3[p]
         tx[p] = total
+        mirrors(p, lambda copy: copy.start())
         tt[p] = total.T
-        spread(p, lambda copy: copy.start())
+        lines(p, lambda copy: copy.start())
 
         @pl.when((y + kept) % 8 == aa)
         def _():
@@ -272,6 +276,8 @@
     for name, *where in ORDER:
         steps[name](*where)
 
+    for c in sent:
+        c.wait_send()
     result = mine[...]
     for i in range(1, 32):
         remote(tt.at[0, pl.ds(0, 16)], gz.at[i], sz.at[0], rz.at[i], aa=right).wait_recv()
@@ -287,9 +293,8 @@
         out[...] += other * scale
 
     for p in range(4):
-        spread(p, lambda copy: copy.wait_send())
-    for c in sent:
-        c.wait_send()
+        mirrors(p, lambda copy: copy.wait_send())
+        lines(p, lambda copy: copy.wait_send())
 
 
 def shards(field, factor):
@@ -306,7 +311,7 @@
     nx, ny = 6 * K, 2 * K * HOPS
     result = pl.pallas_call(
         body,
-        out_shape=jax.ShapeDtypeStruct((16, T), F32),
+        out_shape=pltpu.VMEM((16, T), F32),
         in_specs=[pl.BlockSpec(memory_space=pl.ANY)] * 2,
         out_specs=pl.BlockSpec(memory_space=pltpu.VMEM),
         scratch_shapes=[

time: 59.6 us -> 57.3 us (0.961)
  the two profiles are of different devices: /device:TPU:4 before, /device:TPU:12 now
where the time goes in v3:
time: 57.3 us; the launch traced here: 57.2 us
  Pallas kernels  56.6 us (99%)
  local copies, waits for them, and re-layouts  0.6 us (1%)
    pallas_call x1, Pallas kernels, shards(): pl.pallas_call(body, out_shape=pltpu.VMEM((16, T), F32), in_specs=[pl.Blo...  56.6 us

profile of v3, /device:TPU:12, one launch (start us, length us, event | category | flops | bytes accessed | tf_op | source)
XLA Modules:
  0.0 57.2 jit_solution(12527411699888061005)
XLA Ops:
  0.0 56.6 %shard_map.28 = f32[16,128]{1,0:T(8,128)S(1)} custom-call(f32[24,128,128]{2,1,0:T(8,128)} %refs_0_.1, f32[128,256]{1,0:T(8,128)} %refs_1_.1), custom_call_target="tpu_custom_call" | custom-call | tf_op jit(solution)/shard_map/pallas_call | solution.py:312
  56.6 0.6 %copy.4 = f32[128,16]{0,1:T(8,128)} copy(f32[128,16]{0,1:T(8,128)S(1)} %bitcast.1) | data formatting | bytes 16384

commit v4 on v3

--- a/solution.py
+++ b/solution.py
@@ -25,17 +25,18 @@
 ORDER = (
     ("W",), ("PA", 0), ("SA", 0, 0), ("SA", 0, 1), ("PB", 0), ("SB", 0, 0),
     ("SB", 0, 1), ("PS", 0), ("Z", 0), ("PA", 1), ("PB", 1), ("PS", 1),
-    ("PA", 2), ("SA", 1, 0), ("PB", 2), ("Z", 1), ("SB", 1, 0), ("PS", 2),
-    ("C", 0, 0), ("C", 0, 1), ("Z", 2), ("SA", 1, 1), ("SB", 1, 1), ("C", 1, 0),
-    ("SA", 2, 0), ("T", 0, 0), ("SB", 2, 0), ("T", 0, 1), ("N", 0), ("SA", 2, 1),
-    ("C", 1, 1), ("SB", 2, 1), ("T", 1, 0), ("C", 2, 0), ("H", 0, 0, 1), ("H", 0, 1, 1),
-    ("G", 0, 1), ("C", 2, 1), ("T", 1, 1), ("N", 1), ("H", 1, 0, 1), ("T", 2, 0),
-    ("H", 0, 0, 2), ("H", 0, 1, 2), ("G", 0, 2), ("T", 2, 1), ("N", 2), ("H", 1, 1, 1),
-    ("G", 1, 1), ("H", 1, 0, 2), ("H", 2, 0, 1), ("H", 0, 0, 3), ("H", 0, 1, 3), ("G", 0, 3),
+    ("PA", 2), ("SA", 1, 0), ("PB", 2), ("Z", 1), ("C", 0, 0), ("PS", 2),
+    ("SB", 1, 0), ("C", 0, 1), ("Z", 2), ("SA", 1, 1), ("SB", 1, 1), ("C", 1, 0),
+    ("T", 0, 0), ("SA", 2, 0), ("SB", 2, 0), ("T", 0, 1), ("N", 0), ("SA", 2, 1),
+    ("C", 1, 1), ("H", 0, 0, 1), ("SB", 2, 1), ("T", 1, 0), ("C", 2, 0), ("H", 0, 1, 1),
+    ("G", 0, 1), ("C", 2, 1), ("T", 1, 1), ("N", 1), ("H", 0, 0, 2), ("H", 1, 0, 1),
+    ("T", 2, 0), ("H", 0, 1, 2), ("G", 0, 2), ("T", 2, 1), ("N", 2), ("H", 1, 1, 1),
+    ("G", 1, 1), ("H", 0, 0, 3), ("H", 1, 0, 2), ("H", 2, 0, 1), ("H", 0, 1, 3), ("G", 0, 3),
     ("H", 2, 1, 1), ("G", 2, 1), ("H", 1, 1, 2), ("G", 1, 2), ("H", 1, 0, 3), ("H", 2, 0, 2),
     ("G", 0, 4), ("H", 2, 1, 2), ("G", 2, 2), ("P1", 0), ("P1", 1), ("P2", 0),
-    ("P2", 1), ("G", 1, 3), ("G", 1, 4), ("G", 2, 3), ("G", 2, 4), ("P1", 3),
-    ("P1", 2), ("P2", 3), ("P2", 2),
+    ("P3", 0), ("P2", 1), ("P3", 1), ("G", 1, 3), ("G", 1, 4), ("G", 2, 3),
+    ("G", 2, 4), ("P1", 3), ("P1", 2), ("P2", 3), ("P2", 2), ("P3", 3),
+    ("P3", 2),
 )
 
 
@@ -264,7 +265,10 @@
         total = g[kept] + g3[p]
         tx[p] = total
         mirrors(p, lambda copy: copy.start())
-        tt[p] = total.T
+
+    def step_p3(p):
+        kept = choose(p)[0]
+        tt[p] = tx[p].T
         lines(p, lambda copy: copy.start())
 
         @pl.when((y + kept) % 8 == aa)
@@ -272,7 +276,8 @@
             mine[...] = tt[p, pl.ds(z * 16, 16), :]
 
     steps = {"W": step_w, "PA": step_pa, "PB": step_pb, "PS": step_ps, "SA": step_sa, "SB": step_sb, "C": step_c,
-             "T": step_t, "H": step_h, "N": step_n, "G": step_g, "Z": step_z, "P1": step_p1, "P2": step_p2}
+             "T": step_t, "H": step_h, "N": step_n, "G": step_g, "Z": step_z, "P1": step_p1, "P2": step_p2,
+             "P3": step_p3}
     for name, *where in ORDER:
         steps[name](*where)
 

time: 57.3 us -> 57.3 us (level)
  the two profiles are of different devices: /device:TPU:12 before, /device:TPU:3 now
where the time goes in v4:
time: 57.3 us; the launch traced here: 57.2 us
  Pallas kernels  56.6 us (99%)
  local copies, waits for them, and re-layouts  0.6 us (1%)
    pallas_call x1, Pallas kernels, shards(): pl.pallas_call(body, out_shape=pltpu.VMEM((16, T), F32), in_specs=[pl.Blo...  56.6 us

profile of v4, /device:TPU:3, one launch (start us, length us, event | category | flops | bytes accessed | tf_op | source)
XLA Modules:
  0.0 57.2 jit_solution(5725626227106695820)
XLA Ops:
  0.0 56.6 %shard_map.28 = f32[16,128]{1,0:T(8,128)S(1)} custom-call(f32[24,128,128]{2,1,0:T(8,128)} %refs_0_.1, f32[128,256]{1,0:T(8,128)} %refs_1_.1), custom_call_target="tpu_custom_call" | custom-call | tf_op jit(solution)/shard_map/pallas_call | solution.py:317
  56.6 0.6 %copy.4 = f32[128,16]{0,1:T(8,128)} copy(f32[128,16]{0,1:T(8,128)S(1)} %bitcast.1) | data formatting | bytes 16384
